TPU v7x, 256 devices: a whole 4x4x8 slice. The times are simulated.
256 devices in a mesh: dp: 16 (over z, core), mp: 16 (over y, x).
Axes of the slice: x: 4, y: 4, z: 8, core: 2. Of those that a mesh axis runs over, the one named last changes fastest.
Arguments:
- candidates: bfloat16 [4096, 4096], P('dp', 'mp'), may hold values from -6 to 6
- hold_gate: bfloat16 [4096, 8192], P(None, 'mp'), may hold values from -0.09375 to 0.09375
- hold_up: bfloat16 [4096, 8192], P(None, 'mp'), may hold values from -0.09375 to 0.09375
- probe: float32 [8192], P('mp'), as said below
- chosen: int32 [16, 192], replicated, may hold values from 0 to 4095, as said below
- counts: int32 [16], replicated, may hold values from 24 to 192, as said below
- gate_w: bfloat16 [4096, 14336], P('dp', 'mp'), may hold values from -0.09375 to 0.09375
- up_w: bfloat16 [4096, 14336], P('dp', 'mp'), may hold values from -0.09375 to 0.09375
- cotangent: bfloat16 [3072, 14336], P('dp', 'mp'), may hold values from -6 to 6
Outputs:
- grad_gate: bfloat16 [4096, 14336], P('dp', 'mp')
- grad_up: bfloat16 [4096, 14336], P('dp', 'mp')
- hidden: bfloat16 [3072, 14336], P('dp', 'mp')
- cand_weight: float32 [4096], P('dp')
Inputs may be any that keep to these rules, and one draw needn't show every extreme that they name: `chosen`: all entries are distinct candidate indices. `counts`: exactly one training shard uses all 192 slots in every draw. `probe`: magnitudes at most 12 / sqrt(8192).
All inputs are finite; a program needn't handle non-finite values.
Results may differ from a plain program's by a relative error of at most 0.0057.
Values may be sent and summed in bfloat16 or wider, within the bound.
A program may use at most 128 MiB of HBM per device.

v0:
```python
import jax
import jax.numpy as jnp
from jax import lax
from jax.sharding import PartitionSpec as P


def gather_by_a2a(x, axis_name, axis):
    parts = lax.psum(1, axis_name)
    stacked = lax.all_to_all(
        jnp.broadcast_to(x[None], (parts,) + x.shape),
        axis_name,
        split_axis=0,
        concat_axis=0,
        tiled=True,
    )
    stacked = jnp.moveaxis(stacked, 0, axis)
    shape = list(x.shape)
    shape[axis] *= parts
    return stacked.reshape(shape)


def on_device(candidates, hold_gate, hold_up, probe, chosen, counts, gate_w, up_w, cotangent):
    cand_dev = candidates.shape[0]
    shards = chosen.shape[0]
    slots = chosen.shape[1]
    width = candidates.shape[1]
    ff = gate_w.shape[1]
    merged = lax.all_gather(jnp.concatenate([candidates, gate_w], axis=1), "dp", axis=0, tiled=True)
    all_cands = merged[:, :width]
    full_w = (merged[:, width:], lax.all_gather(up_w, "dp", axis=0, tiled=True))
    own_index = lax.axis_index("dp")
    source = chosen // cand_dev
    local_row = (chosen % cand_dev).reshape(-1)
    valid = jnp.arange(slots, dtype=jnp.int32)[None, :] < counts[:, None]
    usable = (valid & (source == own_index)).reshape(-1)
    onehot = (
        (local_row[:, None] == jnp.arange(cand_dev, dtype=jnp.int32)[None, :]) & usable[:, None]
    ).astype(jnp.bfloat16)
    own_chosen = lax.dynamic_index_in_dim(chosen, own_index, 0, keepdims=False)
    own_valid = lax.dynamic_index_in_dim(valid, own_index, 0, keepdims=False)
    own_onehot = (
        (own_chosen[:, None] == jnp.arange(all_cands.shape[0], dtype=jnp.int32)[None, :])
        & own_valid[:, None]
    ).astype(jnp.bfloat16)
    row_slab = jnp.dot(own_onehot, all_cands, preferred_element_type=jnp.float32).astype(
        jnp.bfloat16
    )
    row_x = gather_by_a2a(row_slab, "mp", 1)
    parts = lax.psum(1, "dp")
    row_blocks = row_x.reshape(row_x.shape[0], parts, -1).transpose(1, 0, 2)
    row_slices = lax.all_to_all(row_blocks, "dp", split_axis=0, concat_axis=0, tiled=True)
    row_slices = row_slices.reshape(-1, row_blocks.shape[2])
    incoming = gather_by_a2a(candidates, "mp", 1)
    hold_g = jnp.dot(incoming, hold_gate, preferred_element_type=jnp.float32)
    hold_u = jnp.dot(incoming, hold_up, preferred_element_type=jnp.float32)
    partial_score = jnp.sum(jax.nn.silu(hold_g) * hold_u * probe[None, :], axis=1)
    score = jnp.sum(gather_by_a2a(partial_score[None, :], "mp", 0), axis=0)
    cand_weight = jax.nn.sigmoid(score)
    picked_weight = (
        jnp.dot(
            onehot, cand_weight.astype(jnp.bfloat16)[:, None], preferred_element_type=jnp.float32
        )
        .astype(jnp.bfloat16)
        .reshape(shards, slots)
    )
    arrived_weight = lax.all_to_all(picked_weight, "dp", split_axis=0, concat_axis=0, tiled=True)
    row_weight = jnp.sum(arrived_weight.astype(jnp.float32), axis=0)
    gate = jnp.dot(row_x, full_w[0], preferred_element_type=jnp.float32)
    up = jnp.dot(row_x, full_w[1], preferred_element_type=jnp.float32)
    hidden = (jax.nn.silu(gate) * up).astype(jnp.bfloat16)
    back = cotangent.astype(jnp.float32) * row_weight[:, None]
    sig = jax.nn.sigmoid(gate)
    d_up = (back * gate * sig).astype(jnp.bfloat16)
    d_gate = (back * up * sig * (1.0 + gate * (1.0 - sig))).astype(jnp.bfloat16)
    contract_rows = (((0,), (0,)), ((), ()))
    d_both, row_slices = lax.optimization_barrier(
        (jnp.concatenate([d_gate, d_up], axis=1), row_slices)
    )
    both_d = lax.all_gather(d_both, "dp", axis=0, tiled=True)
    grads = lax.dot_general(
        row_slices, both_d, contract_rows, preferred_element_type=jnp.float32
    ).astype(jnp.bfloat16)
    return (grads[:, :ff], grads[:, ff:], hidden, cand_weight)


def solution(mesh):
    placed = (
        P("dp", "mp"),
        P(None, "mp"),
        P(None, "mp"),
        P("mp"),
        P(),
        P(),
        P("dp", "mp"),
        P("dp", "mp"),
        P("dp", "mp"),
    )
    return jax.shard_map(
        on_device,
        mesh=mesh,
        in_specs=placed,
        out_specs=(P("dp", "mp"), P("dp", "mp"), P("dp", "mp"), P("dp")),
        check_vma=False,
    )
```

profile of v0, /device:TPU:1, one launch (start us, length us, event | category | flops | bytes accessed | tf_op | source)
XLA Modules:
  0.0 239.8 jit_solution(12118811220462123746)
XLA Ops:
  7.2 1.9 pad_maximum_fusion.1
  10.1 1.5 broadcast_in_dim.6
  11.6 7.7 %all-to-all-start = ((bf16[16,256,256]{1,2,0:T(8,128)(2,1)}), bf16[16,256,256]{1,2,0:T(8,128)(2,1)S(1)}, u32[]{:S(2)}, u32[]{:S(2)}) async-start(bf16[16,256,256]{1,2,0:T(8,128)(2,1)} %broadcast_in_dim.6), calls=%async_computation | async-start | bytes 4194304 | tf_op jit(solution)/shard_map/all_to_all | solution.py:9
  19.4 30.8 %all-to-all-done = bf16[16,256,256]{1,2,0:T(8,128)(2,1)S(1)} async-done(((bf16[16,256,256]{1,2,0:T(8,128)(2,1)}), bf16[16,256,256]{1,2,0:T(8,128)(2,1)S(1)}, u32[]{:S(2)}, u32[]{:S(2)}) %all-to-all-start) | async-done | bytes 2097184 | tf_op jit(solution)/shard_map/all_to_all | solution.py:9
  50.3 3.7 %fusion.26 = f32[256,512]{1,0:T(8,128)S(1)} fusion(bf16[256,4096]{0,1:T(8,128)(2,1)S(1)} %bitcast.20, bf16[4096,512]{1,0:T(8,128)(2,1)} %param.10), kind=kOutput, calls=%fused_computation.42 | convolution fusion | flops 1073741824 | bytes 6815744 | tf_op jit(solution)/shard_map/dot_general | solution.py:54
  54.0 1.4 fusion.14
  56.0 3.9 %all-to-all-start.1 = ((f32[16,1,256]{2,1,0:T(1,128)}), f32[16,1,256]{2,1,0:T(1,128)S(1)}, u32[]{:S(2)}, u32[]{:S(2)}) async-start(f32[16,1,256]{2,1,0:T(1,128)} %broadcast_in_dim.7), calls=%async_computation.1 | async-start | bytes 32768 | tf_op jit(solution)/shard_map/all_to_all | solution.py:9
  60.1 6.2 %all-to-all-done.1 = f32[16,1,256]{2,1,0:T(1,128)S(1)} async-done(((f32[16,1,256]{2,1,0:T(1,128)}), f32[16,1,256]{2,1,0:T(1,128)S(1)}, u32[]{:S(2)}, u32[]{:S(2)}) %all-to-all-start.1) | async-done | bytes 16416 | tf_op jit(solution)/shard_map/all_to_all | solution.py:9
  66.9 2.5 %fusion.6 = f32[1,3072]{1,0:T(1,128)S(1)} fusion(bf16[256,1]{0,1:T(2,128)(2,1)S(1)} %reshape.45, s32[3072]{0:T(1024)S(1)} %eq.38, pred[3072]{0:T(1024)(128)(4,1)S(1)} %and.37), kind=kOutput, calls=%fused_computation.7 | convolution fusion | flops 3145728 | bytes 28160 | tf_op jit(solution)/shard_map/dot_general | solution.py:60
  69.4 0.7 all_to_all.24
  70.1 11.0 %all-to-all-start.2 = ((bf16[16,1,192]{2,1,0:T(2,128)(2,1)}), bf16[16,1,192]{2,1,0:T(2,128)(2,1)S(1)}, u32[]{:S(2)}, u32[]{:S(2)}) async-start(bf16[16,1,192]{2,1,0:T(2,128)(2,1)} %all_to_all.24), calls=%async_computation.2 | async-start | bytes 32768 | tf_op jit(solution)/shard_map/all_to_all | solution.py:66
  81.2 2.4 fusion.15
  83.5 4.9 %all-to-all-done.2 = bf16[16,1,192]{2,1,0:T(2,128)(2,1)S(1)} async-done(((bf16[16,1,192]{2,1,0:T(2,128)(2,1)}), bf16[16,1,192]{2,1,0:T(2,128)(2,1)S(1)}, u32[]{:S(2)}, u32[]{:S(2)}) %all-to-all-start.2) | async-done | bytes 6176 | tf_op jit(solution)/shard_map/all_to_all | solution.py:66
  88.6 25.6 %all_to_all.30 = bf16[16,192,256]{2,1,0:T(8,128)(2,1)} all-to-all(bf16[16,192,256]{2,1,0:T(8,128)(2,1)S(1)} %broadcast_in_dim.8), channel_id=1, replica_groups=mesh['dp'=16,'mp'=16] {'mp'}, dimensions={0} | all-to-all | bytes 3145728 | tf_op jit(solution)/shard_map/all_to_all | solution.py:9
  114.2 5.0 %all-to-all-start.4 = ((bf16[16,192,256]{2,1,0:T(8,128)(2,1)}), bf16[16,192,256]{2,1,0:T(8,128)(2,1)S(1)}, u32[]{:S(2)}, u32[]{:S(2)}) async-start(bf16[16,192,256]{2,1,0:T(8,128)(2,1)} %all_to_all.30), calls=%async_computation.4 | async-start | bytes 3145728 | tf_op jit(solution)/shard_map/all_to_all | solution.py:51
  119.3 1.6 copy.27
  121.0 5.9 %fusion = f32[192,896]{1,0:T(8,128)} fusion(bf16[192,4096]{1,0:T(8,128)(2,1)S(1)} %bitcast.22, bf16[4096,1152]{1,0:T(8,128)(2,1)} %all-gather.4.cloned.1.call-done), kind=kOutput, calls=%fused_computation | convolution fusion | flops 1409286144 | bytes 9601024 | tf_op jit(solution)/shard_map/dot_general | solution.py:68
  126.9 1.1 all-gather.6.cloned.1.call-done
  128.0 5.9 %multiply_convert_fusion = (bf16[192,896]{1,0:T(8,128)(2,1)}, bf16[192,896]{1,0:T(8,128)(2,1)S(1)}, bf16[192,896]{1,0:T(8,128)(2,1)S(1)}) fusion(f32[192,896]{1,0:T(8,128)} %fusion, f32[192]{0:T(256)S(1)} %convert_reduce_fusion, bf16[192,896]{1,0:T(8,128)(2,1)S(1)} %copy-done.4, bf16[192,4096]{1,0:T(8,128)(2,1)S(1)} %bitcast.23, ...), kind=kOutput, calls=%fused_computation.19 | convolution fusion | flops 1412382720 | bytes 10978048 | tf_op jit(solution)/shard_map/dot_general | solution.py:69
  133.9 0.9 pad_maximum_fusion
  134.8 23.4 %all-to-all-done.4 = bf16[16,192,256]{2,1,0:T(8,128)(2,1)S(1)} async-done(((bf16[16,192,256]{2,1,0:T(8,128)(2,1)}), bf16[16,192,256]{2,1,0:T(8,128)(2,1)S(1)}, u32[]{:S(2)}, u32[]{:S(2)}) %all-to-all-start.4) | async-done | bytes 1572896 | tf_op jit(solution)/shard_map/all_to_all | solution.py:51
  158.3 66.9 %all-gather.8.cloned.1.call-done = bf16[3072,1792]{1,0:T(8,128)(2,1)} async-done(((bf16[192,1792]{1,0:T(8,128)(2,1)}), bf16[3072,1792]{1,0:T(8,128)(2,1)}) %all-gather.8.cloned.1.call-update) | async-done | bytes 11010064 | tf_op jit(solution)/shard_map/all_gather | solution.py:79
  225.1 7.2 %convolution_convert_fusion = bf16[256,1792]{1,0:T(8,128)(2,1)S(1)} fusion(bf16[3072,256]{1,0:T(8,128)(2,1)S(1)} %bitcast.19, bf16[3072,1792]{1,0:T(8,128)(2,1)} %all-gather.8.cloned.1.call-done), kind=kOutput, calls=%fused_computation.8 | convolution fusion | flops 2819031040 | bytes 13500416 | tf_op jit(solution)/shard_map/dot_general | solution.py:80
  232.3 1.0 fusion.25
  (33 shorter events, 2.7 us)
Async XLA Ops:
  7.2 2.8 %copy-start = (bf16[256,256]{1,0:T(8,128)(2,1)S(1)}, bf16[256,256]{1,0:T(8,128)(2,1)}, u32[]{:S(2)}) copy-start(bf16[256,256]{1,0:T(8,128)(2,1)} %param.9) | copy-start | bytes 393220
  7.2 74.0 %all-gather.4.cloned.1.call-start = ((), (), s32[]{:S(2)}) async-start(), calls=%async_computation.5 | async-start | bytes 10027008 | tf_op jit(solution)/shard_map/all_gather | solution.py:28
  9.2 118.8 %all-gather.6.cloned.1.call-start = ((), (), s32[]{:S(2)}) async-start(), calls=%async_computation.6 | async-start | bytes 7798784 | tf_op jit(solution)/shard_map/all_gather | solution.py:30
  11.6 7.7 %copy-start.1 = (s32[16,192]{1,0:T(8,128)S(1)}, s32[16,192]{1,0:T(8,128)}, u32[]{:S(2)}) copy-start(s32[16,192]{1,0:T(8,128)} %param.13) | copy-start | bytes 36868
  11.6 7.7 %copy-start.2 = (s32[16]{0:T(128)S(1)}, s32[16]{0:T(128)}, u32[]{:S(2)}) copy-start(s32[16]{0:T(128)} %param.14) | copy-start | bytes 196
  11.6 38.7 %all-to-all-start = ((bf16[16,256,256]{1,2,0:T(8,128)(2,1)}), bf16[16,256,256]{1,2,0:T(8,128)(2,1)S(1)}, u32[]{:S(2)}, u32[]{:S(2)}) async-start(bf16[16,256,256]{1,2,0:T(8,128)(2,1)} %broadcast_in_dim.6), calls=%async_computation | async-start | bytes 4194304 | tf_op jit(solution)/shard_map/all_to_all | solution.py:9
  50.3 3.7 %copy-start.3 = (bf16[4096,512]{1,0:T(8,128)(2,1)S(1)}, bf16[4096,512]{1,0:T(8,128)(2,1)}, u32[]{:S(2)}) copy-start(bf16[4096,512]{1,0:T(8,128)(2,1)} %param.11) | copy-start | bytes 12582916
  50.3 3.7 %copy-start.5 = (f32[512]{0:T(512)S(1)}, f32[512]{0:T(512)}, u32[]{:S(2)}) copy-start(f32[512]{0:T(512)} %param.12) | copy-start | bytes 6148
  56.0 10.3 %all-to-all-start.1 = ((f32[16,1,256]{2,1,0:T(1,128)}), f32[16,1,256]{2,1,0:T(1,128)S(1)}, u32[]{:S(2)}, u32[]{:S(2)}) async-start(f32[16,1,256]{2,1,0:T(1,128)} %broadcast_in_dim.7), calls=%async_computation.1 | async-start | bytes 32768 | tf_op jit(solution)/shard_map/all_to_all | solution.py:9
  70.1 18.3 %all-to-all-start.2 = ((bf16[16,1,192]{2,1,0:T(2,128)(2,1)}), bf16[16,1,192]{2,1,0:T(2,128)(2,1)S(1)}, u32[]{:S(2)}, u32[]{:S(2)}) async-start(bf16[16,1,192]{2,1,0:T(2,128)(2,1)} %all_to_all.24), calls=%async_computation.2 | async-start | bytes 32768 | tf_op jit(solution)/shard_map/all_to_all | solution.py:66
  114.2 44.0 %all-to-all-start.4 = ((bf16[16,192,256]{2,1,0:T(8,128)(2,1)}), bf16[16,192,256]{2,1,0:T(8,128)(2,1)S(1)}, u32[]{:S(2)}, u32[]{:S(2)}) async-start(bf16[16,192,256]{2,1,0:T(8,128)(2,1)} %all_to_all.30), calls=%async_computation.4 | async-start | bytes 3145728 | tf_op jit(solution)/shard_map/all_to_all | solution.py:51
  119.3 105.9 %all-gather.8.cloned.1.call-start = ((), (), s32[]{:S(2)}) async-start(), calls=%async_computation.7 | async-start | bytes 11698176 | tf_op jit(solution)/shard_map/all_gather | solution.py:79
  121.0 7.0 %copy-start.4 = (bf16[192,896]{1,0:T(8,128)(2,1)S(1)}, bf16[192,896]{1,0:T(8,128)(2,1)}, u32[]{:S(2)}) copy-start(bf16[192,896]{1,0:T(8,128)(2,1)} %param.17) | copy-start | bytes 1032196
Sparse Core Ops, SparseCore 0:
  9.8 64.9 all-gather.3
  76.7 51.3 all-gather.5
  158.4 66.7 all-gather.7
where the time goes:
time: 240 us
  waiting for transfers between devices  134 us (56%)
  matrix products  28.9 us (12%)
  starting transfers between devices  27.7 us (12%)
  blocking collectives  25.6 us (11%)
  between operations  13.9 us (6%)
  local copies, waits for them, and re-layouts  5.97 us (2%)
  other arithmetic  3.59 us (1%)
    all_gather x1, waiting for transfers between devices, on_device(): both_d = lax.all_gather(d_both, 'dp', axis=0, tiled=True)  66.9 us
    all_to_all x2, waiting for transfers between devices, gather_by_a2a(): lax.all_to_all(jnp.broadcast_to(x[None], (parts,) + x.shape), axis_name,...  37.1 us
    all_to_all x1, blocking collectives, gather_by_a2a(): lax.all_to_all(jnp.broadcast_to(x[None], (parts,) + x.shape), axis_name,...  25.6 us
    all_to_all x1, waiting for transfers between devices, on_device(): lax.all_to_all(row_blocks, 'dp', split_axis=0, concat_axis=0, tiled=True)  23.4 us
    all_to_all x2, starting transfers between devices, gather_by_a2a(): lax.all_to_all(jnp.broadcast_to(x[None], (parts,) + x.shape), axis_name,...  11.6 us
    all_to_all x1, starting transfers between devices, on_device(): lax.all_to_all(picked_weight, 'dp', split_axis=0, concat_axis=0, tiled=True)  11 us
    dot_general x1, matrix products, on_device(): lax.dot_general(row_slices, both_d, contract_rows, preferred_element_type...  7.17 us
    dot_general x1, matrix products, on_device(): up = jnp.dot(row_x, full_w[1], preferred_element_type=jnp.float32)  5.92 us
  transfers between devices with their start and end apart: 7, of which 6 were waited for; matrix products, arithmetic and copies ran while one was open for 12% of the time, Pallas kernels for 0%

commit v1 on v0

--- a/solution.py
+++ b/solution.py
@@ -76,7 +76,21 @@
     d_both, row_slices = lax.optimization_barrier(
         (jnp.concatenate([d_gate, d_up], axis=1), row_slices)
     )
-    both_d = lax.all_gather(d_both, "dp", axis=0, tiled=True)
+    ways, here, step = (lax.axis_size("dp"), lax.axis_index("dp"), d_both.shape[0])
+    dims = [n * ways if d == 0 else n for d, n in enumerate(d_both.shape)]
+    full = lax.dynamic_update_slice_in_dim(
+        jnp.zeros(dims, d_both.dtype), d_both, here * step, axis=0
+    )
+    going_up = going_down = d_both
+    for far in range(1, ways // 2 + 1):
+        going_up = lax.ppermute(going_up, "dp", [(d, (d + 1) % ways) for d in range(ways)])
+        full = lax.dynamic_update_slice_in_dim(full, going_up, (here - far) % ways * step, axis=0)
+        if 2 * far < ways:
+            going_down = lax.ppermute(going_down, "dp", [(d, (d - 1) % ways) for d in range(ways)])
+            full = lax.dynamic_update_slice_in_dim(
+                full, going_down, (here + far) % ways * step, axis=0
+            )
+    both_d = full
     grads = lax.dot_general(
         row_slices, both_d, contract_rows, preferred_element_type=jnp.float32
     ).astype(jnp.bfloat16)

time: 240 us -> 265 us (1.10)
  the two profiles are of different devices: /device:TPU:1 before, /device:TPU:2 now
where the time goes in v1:
time: 265 us; the launch traced here: 264 us
  waiting for transfers between devices  124 us (47%)
  starting transfers between devices  49.4 us (19%)
  matrix products  28.1 us (11%)
  blocking collectives  26.5 us (10%)
  local copies, waits for them, and re-layouts  17.8 us (7%)
  between operations  14.2 us (5%)
  other arithmetic  4.16 us (2%)
    ppermute x8, waiting for transfers between devices, on_device(): lax.ppermute(going_up, 'dp', [(d, (d + 1) % ways) for d in range(ways)])  56.6 us
    all_to_all x2, waiting for transfers between devices, gather_by_a2a(): lax.all_to_all(jnp.broadcast_to(x[None], (parts,) + x.shape), axis_name,...  31 us
    all_to_all x1, blocking collectives, gather_by_a2a(): lax.all_to_all(jnp.broadcast_to(x[None], (parts,) + x.shape), axis_name,...  26.5 us
    all_to_all x1, waiting for transfers between devices, on_device(): lax.all_to_all(row_blocks, 'dp', split_axis=0, concat_axis=0, tiled=True)  24.3 us
    ppermute x7, starting transfers between devices, on_device(): lax.ppermute(going_down, 'dp', [(d, (d - 1) % ways) for d in range(ways)])  20 us
    all_to_all x2, starting transfers between devices, gather_by_a2a(): lax.all_to_all(jnp.broadcast_to(x[None], (parts,) + x.shape), axis_name,...  15.6 us
    all_to_all x1, starting transfers between devices, on_device(): lax.all_to_all(picked_weight, 'dp', split_axis=0, concat_axis=0, tiled=True)  8.64 us
    dot_general x1, matrix products, on_device(): up = jnp.dot(row_x, full_w[1], preferred_element_type=jnp.float32)  5.87 us
  transfers between devices with their start and end apart: 21, of which 16 were waited for; matrix products, arithmetic and copies ran while one was open for 16% of the time, Pallas kernels for 0%

profile of v1, /device:TPU:2, one launch (start us, length us, event | category | flops | bytes accessed | tf_op | source)
XLA Modules:
  0.0 264.1 jit_solution(128910885240869428)
XLA Ops:
  12.4 7.5 %all-to-all-start = ((bf16[16,256,256]{1,2,0:T(8,128)(2,1)}), bf16[16,256,256]{1,2,0:T(8,128)(2,1)}, u32[]{:S(2)}, u32[]{:S(2)}) async-start(bf16[16,256,256]{1,2,0:T(8,128)(2,1)} %broadcast_in_dim.8), calls=%async_computation | async-start | bytes 4194304 | tf_op jit(solution)/shard_map/all_to_all | solution.py:9
  21.5 25.7 %all-to-all-done = bf16[16,256,256]{1,2,0:T(8,128)(2,1)} async-done(((bf16[16,256,256]{1,2,0:T(8,128)(2,1)}), bf16[16,256,256]{1,2,0:T(8,128)(2,1)}, u32[]{:S(2)}, u32[]{:S(2)}) %all-to-all-start) | async-done | bytes 2097184 | tf_op jit(solution)/shard_map/all_to_all | solution.py:9
  47.2 4.2 %fusion.27 = f32[256,512]{1,0:T(8,128)S(1)} fusion(bf16[256,4096]{0,1:T(8,128)(2,1)} %bitcast.1, bf16[4096,512]{1,0:T(8,128)(2,1)} %param.10), kind=kOutput, calls=%fused_computation.59 | convolution fusion | flops 1073741824 | bytes 6815744 | tf_op jit(solution)/shard_map/dot_general | solution.py:54
  51.4 4.3 %fusion.14 = f32[256]{0:T(256)S(1)} fusion(bf16[256,4096]{0,1:T(8,128)(2,1)} %bitcast.1, bf16[4096,512]{1,0:T(8,128)(2,1)} %param.11, f32[256,512]{1,0:T(8,128)S(1)} %fusion.27, f32[512]{0:T(512)S(1)} %copy-done.2), kind=kOutput, calls=%fused_computation.16 | convolution fusion | flops 1074659072 | bytes 6818816 | tf_op jit(solution)/shard_map/dot_general | solution.py:55
  56.3 8.1 %all-to-all-start.1 = ((f32[16,1,256]{2,1,0:T(1,128)}), f32[16,1,256]{2,1,0:T(1,128)S(1)}, u32[]{:S(2)}, u32[]{:S(2)}) async-start(f32[16,1,256]{2,1,0:T(1,128)} %broadcast_in_dim.9), calls=%async_computation.1 | async-start | bytes 32768 | tf_op jit(solution)/shard_map/all_to_all | solution.py:9
  65.3 5.3 %all-to-all-done.1 = f32[16,1,256]{2,1,0:T(1,128)S(1)} async-done(((f32[16,1,256]{2,1,0:T(1,128)}), f32[16,1,256]{2,1,0:T(1,128)S(1)}, u32[]{:S(2)}, u32[]{:S(2)}) %all-to-all-start.1) | async-done | bytes 16416 | tf_op jit(solution)/shard_map/all_to_all | solution.py:9
  74.5 8.6 %all-to-all-start.2 = ((bf16[16,1,192]{2,1,0:T(2,128)(2,1)}), bf16[16,1,192]{2,1,0:T(2,128)(2,1)S(1)}, u32[]{:S(2)}, u32[]{:S(2)}) async-start(bf16[16,1,192]{2,1,0:T(2,128)(2,1)} %all_to_all.24), calls=%async_computation.2 | async-start | bytes 32768 | tf_op jit(solution)/shard_map/all_to_all | solution.py:66
  85.5 5.4 %all-to-all-done.2 = bf16[16,1,192]{2,1,0:T(2,128)(2,1)S(1)} async-done(((bf16[16,1,192]{2,1,0:T(2,128)(2,1)}), bf16[16,1,192]{2,1,0:T(2,128)(2,1)S(1)}, u32[]{:S(2)}, u32[]{:S(2)}) %all-to-all-start.2) | async-done | bytes 6176 | tf_op jit(solution)/shard_map/all_to_all | solution.py:66
  91.1 26.5 %all_to_all.30 = bf16[16,192,256]{2,1,0:T(8,128)(2,1)} all-to-all(bf16[16,192,256]{2,1,0:T(8,128)(2,1)S(1)} %broadcast_in_dim.10), channel_id=1, replica_groups=mesh['dp'=16,'mp'=16] {'mp'}, dimensions={0} | all-to-all | bytes 3145728 | tf_op jit(solution)/shard_map/all_to_all | solution.py:9
  117.6 4.0 %all-to-all-start.4 = ((bf16[16,192,256]{2,1,0:T(8,128)(2,1)}), bf16[16,192,256]{2,1,0:T(8,128)(2,1)S(1)}, u32[]{:S(2)}, u32[]{:S(2)}) async-start(bf16[16,192,256]{2,1,0:T(8,128)(2,1)} %all_to_all.30), calls=%async_computation.4 | async-start | bytes 3145728 | tf_op jit(solution)/shard_map/all_to_all | solution.py:51
  123.3 5.8 %fusion = f32[192,896]{1,0:T(8,128)} fusion(bf16[192,4096]{1,0:T(8,128)(2,1)S(1)} %bitcast.20, bf16[4096,1152]{1,0:T(8,128)(2,1)} %all-gather.3.cloned.1.call-done), kind=kOutput, calls=%fused_computation | convolution fusion | flops 1409286144 | bytes 9601024 | tf_op jit(solution)/shard_map/dot_general | solution.py:68
  129.1 5.9 %multiply_convert_fusion = (bf16[192,896]{1,0:T(8,128)(2,1)}, bf16[192,896]{1,0:T(8,128)(2,1)S(1)}, bf16[192,896]{1,0:T(8,128)(2,1)S(1)}) fusion(f32[192,896]{1,0:T(8,128)} %fusion, f32[192]{0:T(256)S(1)} %convert_reduce_fusion, bf16[192,896]{1,0:T(8,128)(2,1)S(1)} %copy-done.1, bf16[192,4096]{1,0:T(8,128)(2,1)S(1)} %bitcast.21, ...), kind=kOutput, calls=%fused_computation.19 | convolution fusion | flops 1412382720 | bytes 10978048 | tf_op jit(solution)/shard_map/dot_general | solution.py:69
  135.0 24.3 %all-to-all-done.4 = bf16[16,192,256]{2,1,0:T(8,128)(2,1)S(1)} async-done(((bf16[16,192,256]{2,1,0:T(8,128)(2,1)}), bf16[16,192,256]{2,1,0:T(8,128)(2,1)S(1)}, u32[]{:S(2)}, u32[]{:S(2)}) %all-to-all-start.4) | async-done | bytes 1572896 | tf_op jit(solution)/shard_map/all_to_all | solution.py:51
  162.3 8.7 %collective-permute-done = bf16[192,1792]{1,0:T(8,128)(2,1)} collective-permute-done((bf16[192,1792]{1,0:T(8,128)(2,1)S(1)}, bf16[192,1792]{1,0:T(8,128)(2,1)}, u32[]{:S(2)}, u32[]{:S(2)}) %collective-permute-start) | collective-permute-done | bytes 688160 | tf_op jit(solution)/shard_map/ppermute | solution.py:86
  174.0 8.9 %collective-permute-done.2 = bf16[192,1792]{1,0:T(8,128)(2,1)} collective-permute-done((bf16[192,1792]{1,0:T(8,128)(2,1)}, bf16[192,1792]{1,0:T(8,128)(2,1)}, u32[]{:S(2)}, u32[]{:S(2)}) %collective-permute-start.2) | collective-permute-done | bytes 688160 | tf_op jit(solution)/shard_map/ppermute | solution.py:86
  185.8 8.9 %collective-permute-done.4 = bf16[192,1792]{1,0:T(8,128)(2,1)} collective-permute-done((bf16[192,1792]{1,0:T(8,128)(2,1)}, bf16[192,1792]{1,0:T(8,128)(2,1)}, u32[]{:S(2)}, u32[]{:S(2)}) %collective-permute-start.4) | collective-permute-done | bytes 688160 | tf_op jit(solution)/shard_map/ppermute | solution.py:86
  201.9 4.7 %collective-permute-done.6 = bf16[192,1792]{1,0:T(8,128)(2,1)} collective-permute-done((bf16[192,1792]{1,0:T(8,128)(2,1)}, bf16[192,1792]{1,0:T(8,128)(2,1)}, u32[]{:S(2)}, u32[]{:S(2)}) %collective-permute-start.6) | collective-permute-done | bytes 688160 | tf_op jit(solution)/shard_map/ppermute | solution.py:86
  213.7 4.7 %collective-permute-done.8 = bf16[192,1792]{1,0:T(8,128)(2,1)S(1)} collective-permute-done((bf16[192,1792]{1,0:T(8,128)(2,1)}, bf16[192,1792]{1,0:T(8,128)(2,1)S(1)}, u32[]{:S(2)}, u32[]{:S(2)}) %collective-permute-start.8) | collective-permute-done | bytes 688160 | tf_op jit(solution)/shard_map/ppermute | solution.py:86
  221.0 3.1 %collective-permute-start.11 = (bf16[192,1792]{1,0:T(8,128)(2,1)S(1)}, bf16[192,1792]{1,0:T(8,128)(2,1)S(1)}, u32[]{:S(2)}, u32[]{:S(2)}) collective-permute-start(bf16[192,1792]{1,0:T(8,128)(2,1)S(1)} %collective-permute-done.9), channel_id=1, source_target_pairs={{0,240},{16,0},{32,16},{48,32},{64,48},{80,64},{96,80},{112,96},{1... | collective-permute-start | bytes 2064392 | tf_op jit(solution)/shard_map/ppermute | solution.py:89
  224.2 5.8 %collective-permute-done.10 = bf16[192,1792]{1,0:T(8,128)(2,1)S(1)} collective-permute-done((bf16[192,1792]{1,0:T(8,128)(2,1)S(1)}, bf16[192,1792]{1,0:T(8,128)(2,1)S(1)}, u32[]{:S(2)}, u32[]{:S(2)}) %collective-permute-start.10) | collective-permute-done | bytes 688160 | tf_op jit(solution)/shard_map/ppermute | solution.py:86
  232.6 3.1 %collective-permute-start.13 = (bf16[192,1792]{1,0:T(8,128)(2,1)S(1)}, bf16[192,1792]{1,0:T(8,128)(2,1)S(1)}, u32[]{:S(2)}, u32[]{:S(2)}) collective-permute-start(bf16[192,1792]{1,0:T(8,128)(2,1)S(1)} %collective-permute-done.11), channel_id=1, source_target_pairs={{0,240},{16,0},{32,16},{48,32},{64,48},{80,64},{96,80},{112,96},{1... | collective-permute-start | bytes 2064392 | tf_op jit(solution)/shard_map/ppermute | solution.py:89
  235.8 5.8 %collective-permute-done.12 = bf16[192,1792]{1,0:T(8,128)(2,1)S(1)} collective-permute-done((bf16[192,1792]{1,0:T(8,128)(2,1)S(1)}, bf16[192,1792]{1,0:T(8,128)(2,1)S(1)}, u32[]{:S(2)}, u32[]{:S(2)}) %collective-permute-start.12) | collective-permute-done | bytes 688160 | tf_op jit(solution)/shard_map/ppermute | solution.py:86
  244.2 8.9 %collective-permute-done.14 = bf16[192,1792]{1,0:T(8,128)(2,1)S(1)} collective-permute-done((bf16[192,1792]{1,0:T(8,128)(2,1)S(1)}, bf16[192,1792]{1,0:T(8,128)(2,1)S(1)}, u32[]{:S(2)}, u32[]{:S(2)}) %collective-permute-start.14) | collective-permute-done | bytes 688160 | tf_op jit(solution)/shard_map/ppermute | solution.py:86
  253.2 3.0 %convolution_convert_fusion = bf16[256,1792]{1,0:T(8,128)(2,1)S(1)} fusion(bf16[3072,256]{1,0:T(8,128)(2,1)S(1)} %bitcast.19, bf16[3072,1792]{1,0:T(8,128)(2,1)S(1)} %constant_dynamic-update-slice_fusion), kind=kOutput, calls=%fused_computation.8 | convolution fusion | flops 2819031040 | bytes 13500416 | tf_op jit(solution)/shard_map/dot_general | solution.py:94
  (71 shorter events, 48.3 us)
Async XLA Ops:
  7.2 44.2 %copy-start.2 = (f32[512]{0:T(512)S(1)}, f32[512]{0:T(512)}, u32[]{:S(2)}) copy-start(f32[512]{0:T(512)} %param.12) | copy-start | bytes 6148
  7.2 76.0 %all-gather.3.cloned.1.call-start = ((), (), s32[]{:S(2)}) async-start(), calls=%async_computation.5 | async-start | bytes 10027008 | tf_op jit(solution)/shard_map/all_gather | solution.py:28
  9.2 119.9 %all-gather.5.cloned.1.call-start = ((), (), s32[]{:S(2)}) async-start(), calls=%async_computation.6 | async-start | bytes 7798784 | tf_op jit(solution)/shard_map/all_gather | solution.py:30
  12.4 34.7 %all-to-all-start = ((bf16[16,256,256]{1,2,0:T(8,128)(2,1)}), bf16[16,256,256]{1,2,0:T(8,128)(2,1)}, u32[]{:S(2)}, u32[]{:S(2)}) async-start(bf16[16,256,256]{1,2,0:T(8,128)(2,1)} %broadcast_in_dim.8), calls=%async_computation | async-start | bytes 4194304 | tf_op jit(solution)/shard_map/all_to_all | solution.py:9
  56.3 14.3 %all-to-all-start.1 = ((f32[16,1,256]{2,1,0:T(1,128)}), f32[16,1,256]{2,1,0:T(1,128)S(1)}, u32[]{:S(2)}, u32[]{:S(2)}) async-start(f32[16,1,256]{2,1,0:T(1,128)} %broadcast_in_dim.9), calls=%async_computation.1 | async-start | bytes 32768 | tf_op jit(solution)/shard_map/all_to_all | solution.py:9
  74.5 16.5 %all-to-all-start.2 = ((bf16[16,1,192]{2,1,0:T(2,128)(2,1)}), bf16[16,1,192]{2,1,0:T(2,128)(2,1)S(1)}, u32[]{:S(2)}, u32[]{:S(2)}) async-start(bf16[16,1,192]{2,1,0:T(2,128)(2,1)} %all_to_all.24), calls=%async_computation.2 | async-start | bytes 32768 | tf_op jit(solution)/shard_map/all_to_all | solution.py:66
  117.6 11.5 %copy-start.1 = (bf16[192,896]{1,0:T(8,128)(2,1)S(1)}, bf16[192,896]{1,0:T(8,128)(2,1)}, u32[]{:S(2)}) copy-start(bf16[192,896]{1,0:T(8,128)(2,1)} %param.17) | copy-start | bytes 1032196
  117.6 41.7 %all-to-all-start.4 = ((bf16[16,192,256]{2,1,0:T(8,128)(2,1)}), bf16[16,192,256]{2,1,0:T(8,128)(2,1)S(1)}, u32[]{:S(2)}, u32[]{:S(2)}) async-start(bf16[16,192,256]{2,1,0:T(8,128)(2,1)} %all_to_all.30), calls=%async_computation.4 | async-start | bytes 3145728 | tf_op jit(solution)/shard_map/all_to_all | solution.py:51
  135.0 59.7 %copy-start = (bf16[192,1792]{1,0:T(8,128)(2,1)}, bf16[192,1792]{1,0:T(8,128)(2,1)S(1)}, u32[]{:S(2)}) copy-start(bf16[192,1792]{1,0:T(8,128)(2,1)S(1)} %pad_maximum_fusion) | copy-start | bytes 2064388
  159.3 11.7 %collective-permute-start = (bf16[192,1792]{1,0:T(8,128)(2,1)S(1)}, bf16[192,1792]{1,0:T(8,128)(2,1)}, u32[]{:S(2)}, u32[]{:S(2)}) collective-permute-start(bf16[192,1792]{1,0:T(8,128)(2,1)S(1)} %pad_maximum_fusion), channel_id=1, source_target_pairs={{0,16},{16,32},{32,48},{48,64},{64,80},{80,96},{96,112},{112,128},... | collective-permute-start | bytes 2064392 | tf_op jit(solution)/shard_map/ppermute | solution.py:86
  160.4 10.6 %collective-permute-start.1 = (bf16[192,1792]{1,0:T(8,128)(2,1)S(1)}, bf16[192,1792]{1,0:T(8,128)(2,1)}, u32[]{:S(2)}, u32[]{:S(2)}) collective-permute-start(bf16[192,1792]{1,0:T(8,128)(2,1)S(1)} %pad_maximum_fusion), channel_id=1, source_target_pairs={{0,240},{16,0},{32,16},{48,32},{64,48},{80,64},{96,80},{112,96},{1... | collective-permute-start | bytes 2064392 | tf_op jit(solution)/shard_map/ppermute | solution.py:89
  171.0 11.9 %collective-permute-start.2 = (bf16[192,1792]{1,0:T(8,128)(2,1)}, bf16[192,1792]{1,0:T(8,128)(2,1)}, u32[]{:S(2)}, u32[]{:S(2)}) collective-permute-start(bf16[192,1792]{1,0:T(8,128)(2,1)} %collective-permute-done), channel_id=1, source_target_pairs={{0,16},{16,32},{32,48},{48,64},{64,80},{80,96},{96,112},{112,128},... | collective-permute-start | bytes 2064392 | tf_op jit(solution)/shard_map/ppermute | solution.py:86
  171.0 11.9 %collective-permute-start.3 = (bf16[192,1792]{1,0:T(8,128)(2,1)}, bf16[192,1792]{1,0:T(8,128)(2,1)}, u32[]{:S(2)}, u32[]{:S(2)}) collective-permute-start(bf16[192,1792]{1,0:T(8,128)(2,1)} %collective-permute-done.1), channel_id=1, source_target_pairs={{0,240},{16,0},{32,16},{48,32},{64,48},{80,64},{96,80},{112,96},{1... | collective-permute-start | bytes 2064392 | tf_op jit(solution)/shard_map/ppermute | solution.py:89
  182.9 11.9 %collective-permute-start.4 = (bf16[192,1792]{1,0:T(8,128)(2,1)}, bf16[192,1792]{1,0:T(8,128)(2,1)}, u32[]{:S(2)}, u32[]{:S(2)}) collective-permute-start(bf16[192,1792]{1,0:T(8,128)(2,1)} %collective-permute-done.2), channel_id=1, source_target_pairs={{0,16},{16,32},{32,48},{48,64},{64,80},{80,96},{96,112},{112,128},... | collective-permute-start | bytes 2064392 | tf_op jit(solution)/shard_map/ppermute | solution.py:86
  182.9 14.9 %collective-permute-start.5 = (bf16[192,1792]{1,0:T(8,128)(2,1)}, bf16[192,1792]{1,0:T(8,128)(2,1)}, u32[]{:S(2)}, u32[]{:S(2)}) collective-permute-start(bf16[192,1792]{1,0:T(8,128)(2,1)} %collective-permute-done.3), channel_id=1, source_target_pairs={{0,240},{16,0},{32,16},{48,32},{64,48},{80,64},{96,80},{112,96},{1... | collective-permute-start | bytes 2064392 | tf_op jit(solution)/shard_map/ppermute | solution.py:89
  194.8 11.9 %collective-permute-start.6 = (bf16[192,1792]{1,0:T(8,128)(2,1)}, bf16[192,1792]{1,0:T(8,128)(2,1)}, u32[]{:S(2)}, u32[]{:S(2)}) collective-permute-start(bf16[192,1792]{1,0:T(8,128)(2,1)} %collective-permute-done.4), channel_id=1, source_target_pairs={{0,16},{16,32},{32,48},{48,64},{64,80},{80,96},{96,112},{112,128},... | collective-permute-start | bytes 2064392 | tf_op jit(solution)/shard_map/ppermute | solution.py:86
  197.8 11.7 %collective-permute-start.7 = (bf16[192,1792]{1,0:T(8,128)(2,1)}, bf16[192,1792]{1,0:T(8,128)(2,1)S(1)}, u32[]{:S(2)}, u32[]{:S(2)}) collective-permute-start(bf16[192,1792]{1,0:T(8,128)(2,1)} %collective-permute-done.5), channel_id=1, source_target_pairs={{0,240},{16,0},{32,16},{48,32},{64,48},{80,64},{96,80},{112,96},{1... | collective-permute-start | bytes 2064392 | tf_op jit(solution)/shard_map/ppermute | solution.py:89
  206.7 11.8 %collective-permute-start.8 = (bf16[192,1792]{1,0:T(8,128)(2,1)}, bf16[192,1792]{1,0:T(8,128)(2,1)S(1)}, u32[]{:S(2)}, u32[]{:S(2)}) collective-permute-start(bf16[192,1792]{1,0:T(8,128)(2,1)} %collective-permute-done.6), channel_id=1, source_target_pairs={{0,16},{16,32},{32,48},{48,64},{64,80},{80,96},{96,112},{112,128},... | collective-permute-start | bytes 2064392 | tf_op jit(solution)/shard_map/ppermute | solution.py:86
  209.6 11.5 %collective-permute-start.9 = (bf16[192,1792]{1,0:T(8,128)(2,1)S(1)}, bf16[192,1792]{1,0:T(8,128)(2,1)S(1)}, u32[]{:S(2)}, u32[]{:S(2)}) collective-permute-start(bf16[192,1792]{1,0:T(8,128)(2,1)S(1)} %collective-permute-done.7), channel_id=1, source_target_pairs={{0,240},{16,0},{32,16},{48,32},{64,48},{80,64},{96,80},{112,96},{1... | collective-permute-start | bytes 2064392 | tf_op jit(solution)/shard_map/ppermute | solution.py:89
  218.4 11.6 %collective-permute-start.10 = (bf16[192,1792]{1,0:T(8,128)(2,1)S(1)}, bf16[192,1792]{1,0:T(8,128)(2,1)S(1)}, u32[]{:S(2)}, u32[]{:S(2)}) collective-permute-start(bf16[192,1792]{1,0:T(8,128)(2,1)S(1)} %collective-permute-done.8), channel_id=1, source_target_pairs={{0,16},{16,32},{32,48},{48,64},{64,80},{80,96},{96,112},{112,128},... | collective-permute-start | bytes 2064392 | tf_op jit(solution)/shard_map/ppermute | solution.py:86
  221.0 11.6 %collective-permute-start.11 = (bf16[192,1792]{1,0:T(8,128)(2,1)S(1)}, bf16[192,1792]{1,0:T(8,128)(2,1)S(1)}, u32[]{:S(2)}, u32[]{:S(2)}) collective-permute-start(bf16[192,1792]{1,0:T(8,128)(2,1)S(1)} %collective-permute-done.9), channel_id=1, source_target_pairs={{0,240},{16,0},{32,16},{48,32},{64,48},{80,64},{96,80},{112,96},{1... | collective-permute-start | bytes 2064392 | tf_op jit(solution)/shard_map/ppermute | solution.py:89
  230.0 11.6 %collective-permute-start.12 = (bf16[192,1792]{1,0:T(8,128)(2,1)S(1)}, bf16[192,1792]{1,0:T(8,128)(2,1)S(1)}, u32[]{:S(2)}, u32[]{:S(2)}) collective-permute-start(bf16[192,1792]{1,0:T(8,128)(2,1)S(1)} %collective-permute-done.10), channel_id=1, source_target_pairs={{0,16},{16,32},{32,48},{48,64},{64,80},{80,96},{96,112},{112,128},... | collective-permute-start | bytes 2064392 | tf_op jit(solution)/shard_map/ppermute | solution.py:86
  232.6 11.6 %collective-permute-start.13 = (bf16[192,1792]{1,0:T(8,128)(2,1)S(1)}, bf16[192,1792]{1,0:T(8,128)(2,1)S(1)}, u32[]{:S(2)}, u32[]{:S(2)}) collective-permute-start(bf16[192,1792]{1,0:T(8,128)(2,1)S(1)} %collective-permute-done.11), channel_id=1, source_target_pairs={{0,240},{16,0},{32,16},{48,32},{64,48},{80,64},{96,80},{112,96},{1... | collective-permute-start | bytes 2064392 | tf_op jit(solution)/shard_map/ppermute | solution.py:89
  241.6 11.6 %collective-permute-start.14 = (bf16[192,1792]{1,0:T(8,128)(2,1)S(1)}, bf16[192,1792]{1,0:T(8,128)(2,1)S(1)}, u32[]{:S(2)}, u32[]{:S(2)}) collective-permute-start(bf16[192,1792]{1,0:T(8,128)(2,1)S(1)} %collective-permute-done.12), channel_id=1, source_target_pairs={{0,16},{16,32},{32,48},{48,64},{64,80},{80,96},{96,112},{112,128},... | collective-permute-start | bytes 2064392 | tf_op jit(solution)/shard_map/ppermute | solution.py:86
Sparse Core Ops, SparseCore 0:
  9.8 63.7 all-gather.2
  75.4 49.6 all-gather.4
